TPU v7x, 256 devices: a whole 4x4x8 slice. The times are simulated.
256 devices in a mesh: seq: 64 (over x, z, core), head: 4 (over y).
Axes of the slice: x: 4, y: 4, z: 8, core: 2. Of those that a mesh axis runs over, the one named last changes fastest.
Arguments:
- queries: bfloat16 [32768, 4096], P('seq', 'head'), may hold values from -6 to 6
- key_input: bfloat16 [32768, 4096], P('seq', 'head'), may hold values from -6 to 6
- value_input: bfloat16 [32768, 4096], P('seq', 'head'), may hold values from -40 to 40
- gate_input: bfloat16 [32768, 4096], P('seq', 'head'), may hold values from -8 to 8
- kv_state: float32 [32, 128, 128], P('head'), may hold values from -512 to 512
- norm_gain: float32 [4096], replicated, may hold values from 0.25 to 1.75
- out_weight: bfloat16 [4096, 4096], P('head', 'seq'), may hold values from -0.09375 to 0.09375
Outputs:
- output: bfloat16 [32768, 4096], P(('seq', 'head'))
All inputs are finite; a program needn't handle non-finite values.
Results may differ from a plain program's by a relative error of at most 0.02.
Values may be sent and summed in bfloat16 or wider, within the bound.
A program may use at most 128 MiB of HBM per device.

v0:
```python
import jax
import jax.numpy as jnp
from jax import lax
from jax.sharding import PartitionSpec as P

DH = 128
BLOCK = 512
epsilon = 1e-05


def entering(value, axis, join, neutral):
    place = lax.axis_index(axis)
    gathered = lax.all_gather(value.astype(jnp.bfloat16), axis)
    state = jnp.zeros_like(value) + jnp.asarray(neutral, value.dtype)

    def one(turn, state):
        return join(state, lax.dynamic_index_in_dim(gathered, turn, 0, False).astype(value.dtype))

    return lax.fori_loop(0, place, one, state)


def add_states(earlier, later):
    return earlier + later


def gated_norm(attn_rows, gate_rows, gain_part, total_width, square_sum):
    attn_float = attn_rows.astype(jnp.float32)
    scale = lax.rsqrt(square_sum / total_width + epsilon)
    normed = attn_float * scale[:, None] * gain_part[None, :]
    return (normed * jax.nn.sigmoid(gate_rows.astype(jnp.float32))).astype(jnp.bfloat16)


def shards(queries, key_input, value_input, gate_input, kv_state, norm_gain, out_weight):
    tok_rows = queries.shape[0]
    local_width = queries.shape[1]
    local_heads = local_width // DH
    num_blocks = tok_rows // BLOCK
    block_shape = (num_blocks, BLOCK, local_heads, DH)
    q_blocks = queries.reshape(block_shape)
    k_blocks = key_input.reshape(block_shape)
    v_blocks = value_input.reshape(block_shape)
    block_states = jnp.einsum(
        "nthd,nthe->nhde", k_blocks, v_blocks, preferred_element_type=jnp.float32
    )
    own_total = jnp.sum(block_states, axis=0)
    prefix = entering(own_total, "seq", add_states, jnp.zeros_like(own_total))
    start_state = kv_state + prefix
    running = jnp.cumsum(block_states, axis=0) - block_states
    before = start_state[None] + running
    carried_part = jnp.einsum(
        "nthd,nhde->nthe", q_blocks.astype(jnp.float32), before, precision=lax.Precision.HIGHEST
    )
    scores = jnp.einsum("nthd,nshd->nhts", q_blocks, k_blocks, preferred_element_type=jnp.float32)
    causal = jnp.arange(BLOCK)[:, None] >= jnp.arange(BLOCK)[None, :]
    weights = jnp.where(causal[None, None], scores, 0.0).astype(jnp.bfloat16)
    inner_part = jnp.einsum(
        "nhts,nshe->nthe", weights, v_blocks, preferred_element_type=jnp.float32
    )
    attn = (carried_part + inner_part).astype(jnp.bfloat16).reshape(tok_rows, local_width)
    total_width = local_width * lax.axis_size("head")
    tok_attn, tok_gate = (
        lax.all_to_all(attn, "head", split_axis=0, concat_axis=1, tiled=True),
        lax.all_to_all(gate_input, "head", split_axis=0, concat_axis=1, tiled=True),
    )
    tok_float = tok_attn.astype(jnp.float32)
    normed = gated_norm(
        tok_attn, tok_gate, norm_gain, total_width, jnp.sum(tok_float * tok_float, axis=1)
    )
    hidden = lax.all_to_all(normed, "head", split_axis=1, concat_axis=0, tiled=True)
    terms = jnp.dot(
        hidden,
        lax.all_gather(out_weight, "seq", axis=1, tiled=True),
        preferred_element_type=jnp.float32,
    )
    return lax.psum_scatter(terms.astype(jnp.bfloat16), "head", scatter_dimension=0, tiled=True)


def solution(mesh):
    in_specs = (
        P("seq", "head"),
        P("seq", "head"),
        P("seq", "head"),
        P("seq", "head"),
        P("head", None, None),
        P(),
        P("head", "seq"),
    )
    out_specs = P(("seq", "head"), None)
    return jax.shard_map(shards, mesh=mesh, in_specs=in_specs, out_specs=out_specs, check_vma=False)
```

profile of v0, /device:TPU:1, one launch (start us, length us, event | category | flops | bytes accessed | tf_op | source)
XLA Modules:
  0.0 307.6 jit_solution(3969963221888918470)
XLA Ops:
  6.5 0.0 copy-start
  6.5 0.0 all-gather.6.cloned.1.call-start
  6.5 2.9 fusion.34
  9.4 0.0 all-gather.6.cloned.1.call-update
  9.4 0.0 all-gather.4.cloned.1.call-start
  9.5 0.7 all-gather.4.cloned.1.call-update
  10.2 0.1 iota_compare_fusion
  10.3 103.8 %all-gather.6.cloned.1.call-done = bf16[512,128,128]{2,1,0:T(8,128)(2,1)} async-done(((bf16[8,128,128]{2,1,0:T(8,128)(2,1)}), bf16[512,128,128]{2,1,0:T(8,128)(2,1)}) %all-gather.6.cloned.1.call-update) | async-done | bytes 16777232 | tf_op jit(solution)/shard_map/all_gather | solution.py:13
  114.1 0.0 copy-start.2
  114.1 1.2 while.10
  114.1 1.1 convert_add_fusion.2
  115.3 0.0 copy-done
  115.3 0.0 copy-done.2
  115.3 2.4 fusion.13
  117.7 4.8 %fusion.10 = bf16[1,512,8,128]{1,3,2,0:T(8,128)(2,1)S(1)} fusion(f32[8,128,512]{2,1,0:T(8,128)} %fusion.13, pred[512,512]{1,0:T(8,128)(4,1)S(1)} %iota_compare_fusion, bf16[512,1024]{1,0:T(8,128)(2,1)S(1)} %copy-done, bf16[512,1024]{1,0:T(8,128)(2,1)} %param.11, bf16[512,1024]{1,0:T(8,128)(2,1)} %param.10), kind=kOutput, calls=%fused_computation.15 | convolution fusion | flops 1078984704 | bytes 6553600 | tf_op jit(solution)/shard_map/nhts,nshe->nthe/dot_general | solution.py:56
  122.5 0.3 all_to_all.32
  122.8 0.0 copy-start.1
  122.8 1.1 copy.40
  123.9 4.0 %all-to-all-start = ((bf16[4,128,1024]{1,2,0:T(8,128)(2,1)}), bf16[4,128,1024]{1,2,0:T(8,128)(2,1)S(1)}, u32[]{:S(2)}, u32[]{:S(2)}) async-start(bf16[4,128,1024]{1,2,0:T(8,128)(2,1)} %copy.40), calls=%async_computation | async-start | bytes 2097152 | tf_op jit(solution)/shard_map/all_to_all | solution.py:62
  128.0 1.3 copy.41
  129.3 13.6 %all-to-all-done = bf16[4,128,1024]{1,2,0:T(8,128)(2,1)S(1)} async-done(((bf16[4,128,1024]{1,2,0:T(8,128)(2,1)}), bf16[4,128,1024]{1,2,0:T(8,128)(2,1)S(1)}, u32[]{:S(2)}, u32[]{:S(2)}) %all-to-all-start) | async-done | bytes 1048608 | tf_op jit(solution)/shard_map/all_to_all | solution.py:62
  142.8 3.5 %all-to-all-start.1 = ((bf16[4,128,1024]{1,2,0:T(8,128)(2,1)}), bf16[4,128,1024]{1,2,0:T(8,128)(2,1)S(1)}, u32[]{:S(2)}, u32[]{:S(2)}) async-start(bf16[4,128,1024]{1,2,0:T(8,128)(2,1)} %copy.41), calls=%async_computation.1 | async-start | bytes 2097152 | tf_op jit(solution)/shard_map/all_to_all | solution.py:63
  146.3 0.0 reduce-scatter.2.cloned.1.call-start
  146.4 0.6 fusion.5
  147.0 13.3 %all-to-all-done.1 = bf16[4,128,1024]{1,2,0:T(8,128)(2,1)S(1)} async-done(((bf16[4,128,1024]{1,2,0:T(8,128)(2,1)}), bf16[4,128,1024]{1,2,0:T(8,128)(2,1)S(1)}, u32[]{:S(2)}, u32[]{:S(2)}) %all-to-all-start.1) | async-done | bytes 1048608 | tf_op jit(solution)/shard_map/all_to_all | solution.py:63
  160.2 0.8 fusion.21
  161.0 15.2 %all_to_all.42 = bf16[128,4,1024]{0,2,1:T(8,128)(2,1)S(1)} all-to-all(bf16[128,4,1024]{0,2,1:T(8,128)(2,1)S(1)} %fusion.21), channel_id=1, replica_groups=mesh['seq'=64,'head'=4] {'head'}, dimensions={1} | all-to-all | bytes 2097152 | tf_op jit(solution)/shard_map/all_to_all | solution.py:69
  176.2 0.5 copy.42
  176.7 20.2 %all-gather.4.cloned.1.call-done = bf16[1024,4096]{0,1:T(8,128)(2,1)} async-done(((bf16[1024,64]{0,1:T(8,128)(2,1)}), bf16[1024,4096]{0,1:T(8,128)(2,1)}) %all-gather.4.cloned.1.call-update) | async-done | bytes 8388624 | tf_op jit(solution)/shard_map/all_gather | solution.py:72
  196.9 9.4 %convolution_convert_fusion = bf16[512,4096]{1,0:T(8,128)(2,1)} fusion(bf16[512,1024]{1,0:T(8,128)(2,1)S(1)} %bitcast.73, bf16[1024,4096]{0,1:T(8,128)(2,1)} %all-gather.4.cloned.1.call-done), kind=kOutput, calls=%fused_computation.2 | convolution fusion | flops 4297064448 | bytes 13631488 | tf_op jit(solution)/shard_map/dot_general | solution.py:70
  206.3 0.0 reduce-scatter.2.cloned.1.call-update
  206.4 94.8 %reduce-scatter.2.cloned.1.call-done = bf16[128,4096]{1,0:T(8,128)(2,1)} async-done(((bf16[512,4096]{1,0:T(8,128)(2,1)}), bf16[128,4096]{1,0:T(8,128)(2,1)}) %reduce-scatter.2.cloned.1.call-update) | async-done | bytes 1048592 | tf_op jit(solution)/shard_map/reduce_scatter | solution.py:75
  (6 shorter events, 0.1 us)
Async XLA Ops:
  6.5 108.7 %copy-start = (bf16[512,1024]{1,0:T(8,128)(2,1)S(1)}, bf16[512,1024]{1,0:T(8,128)(2,1)}, u32[]{:S(2)}) copy-start(bf16[512,1024]{1,0:T(8,128)(2,1)} %param.9) | copy-start | bytes 3145732
  6.5 107.5 %all-gather.6.cloned.1.call-start = ((), (), s32[]{:S(2)}) async-start(), calls=%async_computation.6 | async-start | bytes 17039360 | tf_op jit(solution)/shard_map/all_gather | solution.py:13
  9.4 187.4 %all-gather.4.cloned.1.call-start = ((), (), s32[]{:S(2)}) async-start(), calls=%async_computation.4 | async-start | bytes 8519680 | tf_op jit(solution)/shard_map/all_gather | solution.py:72
  114.1 1.2 copy-start.2
  122.8 5.1 %copy-start.1 = (bf16[512,1024]{1,0:T(8,128)(2,1)S(1)}, bf16[512,1024]{1,0:T(8,128)(2,1)}, u32[]{:S(2)}) copy-start(bf16[512,1024]{1,0:T(8,128)(2,1)} %param.12) | copy-start | bytes 3145732
  123.9 18.9 %all-to-all-start = ((bf16[4,128,1024]{1,2,0:T(8,128)(2,1)}), bf16[4,128,1024]{1,2,0:T(8,128)(2,1)S(1)}, u32[]{:S(2)}, u32[]{:S(2)}) async-start(bf16[4,128,1024]{1,2,0:T(8,128)(2,1)} %copy.40), calls=%async_computation | async-start | bytes 2097152 | tf_op jit(solution)/shard_map/all_to_all | solution.py:62
  127.9 18.4 %copy-start.3 = (f32[4096]{0:T(1024)S(1)}, f32[4096]{0:T(1024)}, u32[]{:S(2)}) copy-start(f32[4096]{0:T(1024)} %param.14) | copy-start | bytes 49156
  142.8 17.4 %all-to-all-start.1 = ((bf16[4,128,1024]{1,2,0:T(8,128)(2,1)}), bf16[4,128,1024]{1,2,0:T(8,128)(2,1)S(1)}, u32[]{:S(2)}, u32[]{:S(2)}) async-start(bf16[4,128,1024]{1,2,0:T(8,128)(2,1)} %copy.41), calls=%async_computation.1 | async-start | bytes 2097152 | tf_op jit(solution)/shard_map/all_to_all | solution.py:63
  146.3 154.8 %reduce-scatter.2.cloned.1.call-start = ((), (), s32[]{:S(2)}) async-start(), calls=%async_computation.5 | async-start | bytes 5242880 | tf_op jit(solution)/shard_map/reduce_scatter | solution.py:75
Sparse Core Ops, SparseCore 0:
  10.1 103.8 all-gather.5
  116.8 79.9 all-gather.3
  206.5 94.5 reduce-scatter.1
where the time goes:
time: 310 us; the launch traced here: 308 us
  waiting for transfers between devices  246 us (79%)
  matrix products  19.5 us (6%)
  blocking collectives  15.2 us (5%)
  between operations  13.2 us (4%)
  starting transfers between devices  7.63 us (2%)
  local copies, waits for them, and re-layouts  3.29 us (1%)
    all_gather x1, waiting for transfers between devices, entering(): gathered = lax.all_gather(value.astype(jnp.bfloat16), axis)  104 us
    reduce_scatter x1, waiting for transfers between devices, shards(): lax.psum_scatter(terms.astype(jnp.bfloat16), 'head', scatter_dimension=0,...  94.8 us
    all_gather x1, waiting for transfers between devices, shards(): lax.all_gather(out_weight, 'seq', axis=1, tiled=True)  20.2 us
    all_to_all x1, blocking collectives, shards(): lax.all_to_all(normed, 'head', split_axis=1, concat_axis=0, tiled=True)  15.2 us
    all_to_all x1, waiting for transfers between devices, shards(): lax.all_to_all(attn, 'head', split_axis=0, concat_axis=1, tiled=True)  13.6 us
    all_to_all x1, waiting for transfers between devices, shards(): lax.all_to_all(gate_input, 'head', split_axis=0, concat_axis=1, tiled=True)  13.3 us
    dot_general x1, matrix products, shards(): jnp.dot(hidden, lax.all_gather(out_weight, 'seq', axis=1, tiled=True), pr...  9.44 us
  transfers between devices with their start and end apart: 5, of which 5 were waited for; matrix products, arithmetic and copies ran while one was open for 4% of the time, Pallas kernels for 0%

commit v1 on v0

--- a/solution.py
+++ b/solution.py
@@ -66,7 +66,10 @@
     normed = gated_norm(
         tok_attn, tok_gate, norm_gain, total_width, jnp.sum(tok_float * tok_float, axis=1)
     )
-    hidden = lax.all_to_all(normed, "head", split_axis=1, concat_axis=0, tiled=True)
+    hidden = jnp.concatenate(
+        lax.all_to_all(jnp.stack(jnp.split(normed, lax.axis_size("head"), axis=1)), "head", 0, 0),
+        axis=0,
+    )
     terms = jnp.dot(
         hidden,
         lax.all_gather(out_weight, "seq", axis=1, tiled=True),

time: 310 us -> 297 us (0.958)
  waiting for transfers between devices: 246 us -> 222 us
  other arithmetic: 2.52 us -> 5.67 us
    all_to_all x1, waiting for transfers between devices: 13.3 us -> 0.01 us  [shards(): lax.all_to_all(gate_input, 'head', split_axis=0, concat_axis=1, tiled=True)]
    reduce_scatter x1, waiting for transfers between devices: 94.8 us -> 81.5 us  [shards(): lax.psum_scatter(terms.astype(jnp.bfloat16), 'head', scatter_dimension=0,...]
    all_gather x1, waiting for transfers between devices: 20.2 us -> 30 us  [shards(): lax.all_gather(out_weight, 'seq', axis=1, tiled=True)]
    all_gather x1, waiting for transfers between devices: 104 us -> 98.8 us  [entering(): gathered = lax.all_gather(value.astype(jnp.bfloat16), axis)]
  transfers between devices with their start and end apart: 5 -> 5, of which waited for: 5 -> 4; matrix products, arithmetic and copies ran while one was open for 4% -> 7% of each run, Pallas kernels for 0% -> 0%
where the time goes in v1:
time: 297 us; the launch traced here: 294 us
  waiting for transfers between devices  222 us (75%)
  matrix products  21.5 us (7%)
  blocking collectives  17.2 us (6%)
  between operations  13.2 us (4%)
  starting transfers between devices  9.06 us (3%)
  local copies, waits for them, and re-layouts  6.02 us (2%)
  other arithmetic  5.67 us (2%)
    all_gather x1, waiting for transfers between devices, entering(): gathered = lax.all_gather(value.astype(jnp.bfloat16), axis)  98.8 us
    reduce_scatter x1, waiting for transfers between devices, shards(): lax.psum_scatter(terms.astype(jnp.bfloat16), 'head', scatter_dimension=0,...  81.5 us
    all_gather x1, waiting for transfers between devices, shards(): lax.all_gather(out_weight, 'seq', axis=1, tiled=True)  30 us
    all_to_all x1, blocking collectives, shards(): lax.all_to_all(jnp.stack(jnp.split(normed, lax.axis_size('head'), axis=1)...  17.2 us
    all_to_all x1, waiting for transfers between devices, shards(): lax.all_to_all(attn, 'head', split_axis=0, concat_axis=1, tiled=True)  10.6 us
    dot_general x1, matrix products, shards(): jnp.dot(hidden, lax.all_gather(out_weight, 'seq', axis=1, tiled=True), pr...  9.45 us
  transfers between devices with their start and end apart: 5, of which 4 were waited for; matrix products, arithmetic and copies ran while one was open for 7% of the time, Pallas kernels for 0%

profile of v1, /device:TPU:1, one launch (start us, length us, event | category | flops | bytes accessed | tf_op | source)
XLA Modules:
  0.0 294.4 jit_solution(1102798989970370436)
XLA Ops:
  6.5 0.0 copy-start
  6.5 0.0 all-gather.6.cloned.1.call-start
  6.5 2.9 fusion.32
  9.4 0.0 all-gather.6.cloned.1.call-update
  9.4 0.0 all-gather.4.cloned.1.call-start
  9.5 0.7 all-gather.4.cloned.1.call-update
  10.2 5.0 %all-to-all-start.1 = ((bf16[4,128,1024]{2,1,0:T(8,128)(2,1)}), bf16[4,128,1024]{2,1,0:T(8,128)(2,1)S(1)}, u32[]{:S(2)}, u32[]{:S(2)}) async-start(bf16[4,128,1024]{2,1,0:T(8,128)(2,1)} %bitcast.90), calls=%async_computation.1 | async-start | bytes 2097152 | tf_op jit(solution)/shard_map/all_to_all | solution.py:63
  15.2 0.1 iota_compare_fusion
  15.3 98.8 %all-gather.6.cloned.1.call-done = bf16[512,128,128]{2,1,0:T(8,128)(2,1)} async-done(((bf16[8,128,128]{2,1,0:T(8,128)(2,1)}), bf16[512,128,128]{2,1,0:T(8,128)(2,1)}) %all-gather.6.cloned.1.call-update) | async-done | bytes 16777232 | tf_op jit(solution)/shard_map/all_gather | solution.py:13
  114.1 1.1 while.10
  114.1 1.1 convert_add_fusion.2
  115.2 0.0 copy-done
  115.2 3.4 %fusion.12 = f32[8,128,512]{2,1,0:T(8,128)} fusion(f32[8,128,128]{2,1,0:T(8,128)S(1)} %get-tuple-element.42, f32[8,128,128]{2,1,0:T(8,128)} %param.13, f32[8,128,128]{2,1,0:T(8,128)S(1)} %get-tuple-element.28, bf16[512,1024]{1,0:T(8,128)(2,1)S(1)} %copy-done), kind=kOutput, calls=%fused_computation.17 | convolution fusion | flops 805699584 | bytes 4718592 | tf_op jit(solution)/shard_map/nthd,nhde->nthe/dot_general | solution.py:50
  118.6 5.8 %fusion.9 = bf16[1,512,8,128]{1,3,2,0:T(8,128)(2,1)} fusion(f32[8,128,512]{2,1,0:T(8,128)} %fusion.12, pred[512,512]{1,0:T(8,128)(4,1)S(1)} %iota_compare_fusion, bf16[512,1024]{1,0:T(8,128)(2,1)S(1)} %copy-done, bf16[512,1024]{1,0:T(8,128)(2,1)} %param.11, bf16[512,1024]{1,0:T(8,128)(2,1)} %param.10), kind=kOutput, calls=%fused_computation.15 | convolution fusion | flops 1078984704 | bytes 6553600 | tf_op jit(solution)/shard_map/nhts,nshe->nthe/dot_general | solution.py:56
  124.4 1.4 all_to_all.23
  125.8 1.1 copy.40
  126.9 0.0 all-to-all-done.1
  126.9 4.0 %all-to-all-start = ((bf16[4,128,1024]{1,2,0:T(8,128)(2,1)}), bf16[4,128,1024]{1,2,0:T(8,128)(2,1)S(1)}, u32[]{:S(2)}, u32[]{:S(2)}) async-start(bf16[4,128,1024]{1,2,0:T(8,128)(2,1)} %copy.40), calls=%async_computation | async-start | bytes 2097152 | tf_op jit(solution)/shard_map/all_to_all | solution.py:62
  130.9 0.0 reduce-scatter.2.cloned.1.call-start
  130.9 1.9 divide_bitcast_fusion
  132.8 2.9 copy.41
  135.7 10.6 %all-to-all-done = bf16[4,128,1024]{1,2,0:T(8,128)(2,1)S(1)} async-done(((bf16[4,128,1024]{1,2,0:T(8,128)(2,1)}), bf16[4,128,1024]{1,2,0:T(8,128)(2,1)S(1)}, u32[]{:S(2)}, u32[]{:S(2)}) %all-to-all-start) | async-done | bytes 1048608 | tf_op jit(solution)/shard_map/all_to_all | solution.py:62
  146.3 0.6 multiply_reduce_fusion
  146.9 1.9 fusion.7
  148.9 0.1 slice_bitcast_fusion.3
  148.9 0.1 pad_maximum_fusion
  149.1 17.2 %all_to_all.31 = bf16[4,128,1024]{1,2,0:T(8,128)(2,1)S(1)} all-to-all(bf16[4,128,1024]{1,2,0:T(8,128)(2,1)S(1)} %pad_maximum_fusion), channel_id=1, replica_groups=mesh['seq'=64,'head'=4] {'head'}, dimensions={0} | all-to-all | bytes 2097152 | tf_op jit(solution)/shard_map/all_to_all | solution.py:70
  166.3 0.5 copy.42
  166.9 30.0 %all-gather.4.cloned.1.call-done = bf16[1024,4096]{0,1:T(8,128)(2,1)} async-done(((bf16[1024,64]{0,1:T(8,128)(2,1)}), bf16[1024,4096]{0,1:T(8,128)(2,1)}) %all-gather.4.cloned.1.call-update) | async-done | bytes 8388624 | tf_op jit(solution)/shard_map/all_gather | solution.py:75
  196.9 9.4 %convolution_convert_fusion = bf16[512,4096]{1,0:T(8,128)(2,1)} fusion(bf16[512,1024]{1,0:T(8,128)(2,1)S(1)} %bitcast.91, bf16[1024,4096]{0,1:T(8,128)(2,1)} %all-gather.4.cloned.1.call-done), kind=kOutput, calls=%fused_computation.2 | convolution fusion | flops 4297064448 | bytes 13631488 | tf_op jit(solution)/shard_map/dot_general | solution.py:73
  206.3 0.0 reduce-scatter.2.cloned.1.call-update
  206.4 81.5 %reduce-scatter.2.cloned.1.call-done = bf16[128,4096]{1,0:T(8,128)(2,1)} async-done(((bf16[512,4096]{1,0:T(8,128)(2,1)}), bf16[128,4096]{1,0:T(8,128)(2,1)}) %reduce-scatter.2.cloned.1.call-update) | async-done | bytes 1048592 | tf_op jit(solution)/shard_map/reduce_scatter | solution.py:78
  (4 shorter events, 0.0 us)
Async XLA Ops:
  6.5 108.7 %copy-start = (bf16[512,1024]{1,0:T(8,128)(2,1)S(1)}, bf16[512,1024]{1,0:T(8,128)(2,1)}, u32[]{:S(2)}) copy-start(bf16[512,1024]{1,0:T(8,128)(2,1)} %param.9) | copy-start | bytes 3145732
  6.5 107.5 %all-gather.6.cloned.1.call-start = ((), (), s32[]{:S(2)}) async-start(), calls=%async_computation.6 | async-start | bytes 17039360 | tf_op jit(solution)/shard_map/all_gather | solution.py:13
  9.4 187.4 %all-gather.4.cloned.1.call-start = ((), (), s32[]{:S(2)}) async-start(), calls=%async_computation.4 | async-start | bytes 8519680 | tf_op jit(solution)/shard_map/all_gather | solution.py:75
  10.2 116.7 %all-to-all-start.1 = ((bf16[4,128,1024]{2,1,0:T(8,128)(2,1)}), bf16[4,128,1024]{2,1,0:T(8,128)(2,1)S(1)}, u32[]{:S(2)}, u32[]{:S(2)}) async-start(bf16[4,128,1024]{2,1,0:T(8,128)(2,1)} %bitcast.90), calls=%async_computation.1 | async-start | bytes 2097152 | tf_op jit(solution)/shard_map/all_to_all | solution.py:63
  126.9 19.4 %all-to-all-start = ((bf16[4,128,1024]{1,2,0:T(8,128)(2,1)}), bf16[4,128,1024]{1,2,0:T(8,128)(2,1)S(1)}, u32[]{:S(2)}, u32[]{:S(2)}) async-start(bf16[4,128,1024]{1,2,0:T(8,128)(2,1)} %copy.40), calls=%async_computation | async-start | bytes 2097152 | tf_op jit(solution)/shard_map/all_to_all | solution.py:62
  130.9 157.0 %reduce-scatter.2.cloned.1.call-start = ((), (), s32[]{:S(2)}) async-start(), calls=%async_computation.5 | async-start | bytes 5242880 | tf_op jit(solution)/shard_map/reduce_scatter | solution.py:78
  132.8 14.1 %copy-start.1 = (f32[4096]{0:T(1024)S(1)}, f32[4096]{0:T(1024)}, u32[]{:S(2)}) copy-start(f32[4096]{0:T(1024)} %param.14) | copy-start | bytes 49156
Sparse Core Ops, SparseCore 0:
  10.1 103.8 all-gather.5
  116.8 80.0 all-gather.3
  206.5 81.3 reduce-scatter.1
